TPU v7x, 256 devices: a whole 4x4x8 slice. The times are simulated.
256 devices in a mesh: grid: 128 (over x, z, y), rep: 2 (over core).
Axes of the slice: x: 4, y: 4, z: 8, core: 2. Of those that a mesh axis runs over, the one named last changes fastest.
Arguments:
- density_blocks: bfloat16 [3584, 4, 128, 128], P('grid'), may hold values from -0.046875 to 0.046875
- neighbours: int32 [3584, 4], P('grid'), may hold values from 0 to 3583, as said below
- relevant: int32 [3072, 8], P(('grid', 'rep')), may hold values from 0 to 3583, as said below
- batch_count: int32 [256], P(('grid', 'rep')), may hold values from 1 to 12, as said below
- basis_values: bfloat16 [3072, 8, 128, 128], P(('grid', 'rep')), may hold values from -6 to 6
- becke_weights: bfloat16 [3072, 128], P(('grid', 'rep')), may hold values from 0.0039978027 to 0.099609375
Outputs:
- xc_blocks: bfloat16 [3584, 4, 128, 128], P('grid')
Inputs may be any that keep to these rules, and one draw needn't show every extreme that they name: neighbours[a, 0] = a; the 4 column groups of a row group are distinct and lie within 12 consecutive groups that contain a. `relevant`: the 8 groups of a batch are distinct and lie within 12 consecutive groups around a group owned by the batch's grid index; none lies more than 6 groups before the first or after the last group owned by that grid index. `batch_count`: some device has all 12 slots live in every draw.
All inputs are finite; a program needn't handle non-finite values.
Results may differ from a plain program's by a relative error of at most 0.0049.
Values may be sent and summed in bfloat16 or wider, within the bound.
A program may use at most 192 MiB of HBM per device.

v0:
```python
import jax
import jax.numpy as jnp
from jax import lax
from jax.sharding import PartitionSpec as P

SPAN = 12
slater_coef = 0.9847450218426965


def shifted(block, axis, distance):
    devices = range(lax.axis_size(axis))
    route = [(i - distance, i) for i in devices if i - distance in devices]
    return lax.ppermute(block, axis, route)


def in_blocks(array, dim, count):
    before, after = (array.shape[:dim], array.shape[dim + 1 :])
    return jnp.moveaxis(array.reshape(*before, count, -1, *after), dim, 0)


def sum_at_owner(array, axis, dim):
    count = lax.axis_size(axis)
    pieces = lax.all_to_all(in_blocks(array, dim, count), axis, 0, 0, tiled=True)
    return jnp.sum(pieces, axis=0)


def potential(density_at):
    return -slater_coef * density_at * (density_at * density_at + 1.0) ** (-1.0 / 3.0)


def batch_terms(slabs, slab_neighbours, groups, basis_vals, weight_row):
    matches = (slab_neighbours[:, :, None] == groups[None, None, :]).astype(jnp.bfloat16)
    column_basis = jnp.einsum(
        "ikj,jnp->iknp", matches, basis_vals, preferred_element_type=jnp.float32
    ).astype(jnp.bfloat16)
    spread = jnp.einsum("ikmn,iknp->imp", slabs, column_basis, preferred_element_type=jnp.float32)
    basis_wide = basis_vals.astype(jnp.float32)
    density_at = jnp.sum(basis_wide * spread, axis=(0, 1))
    scaled = (
        basis_wide * (weight_row.astype(jnp.float32) * potential(density_at))[None, None, :]
    ).astype(jnp.bfloat16)
    column_scaled = jnp.einsum(
        "ikj,jnp->iknp", matches, scaled, preferred_element_type=jnp.float32
    ).astype(jnp.bfloat16)
    return jnp.einsum(
        "imp,iknp->ikmn", basis_vals, column_scaled, preferred_element_type=jnp.float32
    )


def shards(density_blocks, neighbours, relevant, batch_count, basis_values, becke_weights):
    group_count = density_blocks.shape[0]
    reach = SPAN // 2
    arrived = []
    for offset, low_edge in ((1, group_count - reach), (-1, 0)):
        arrived.append(
            shifted(
                (
                    density_blocks[low_edge : low_edge + reach],
                    neighbours[low_edge : low_edge + reach],
                ),
                "grid",
                offset,
            )
        )
    before_blocks, before_lists = arrived[0]
    after_blocks, after_lists = arrived[1]
    window_blocks = jnp.concatenate([before_blocks, density_blocks, after_blocks], axis=0)
    window_lists = jnp.concatenate([before_lists, neighbours, after_lists], axis=0)
    window_base = lax.axis_index("grid") * group_count - reach
    loop_count = batch_count[0]
    source_groups, source_basis, source_weights = (relevant, basis_values, becke_weights)

    def visit(step_index, buffer):
        groups = source_groups[step_index]
        local_rows = groups - window_base
        blocks = batch_terms(
            window_blocks[local_rows],
            window_lists[local_rows],
            groups,
            source_basis[step_index],
            source_weights[step_index],
        )
        return buffer.at[local_rows].add(blocks)

    start_buffer = jnp.zeros((group_count + 2 * reach,) + density_blocks.shape[1:], jnp.float32)
    buffer = lax.fori_loop(0, loop_count, visit, start_buffer)
    halves = sum_at_owner(buffer, "rep", 1)
    owned_half = halves[reach : reach + group_count]
    gained = []
    for offset, low_edge in ((1, reach + group_count), (-1, 0)):
        gained.append(shifted(halves[low_edge : low_edge + reach], "grid", offset))
    owned_half = owned_half.at[:reach].add(gained[0])
    owned_half = owned_half.at[group_count - reach :].add(gained[1])
    return lax.all_gather(owned_half.astype(jnp.bfloat16), "rep", axis=1, tiled=True)


def solution(mesh):
    placed = (
        P("grid", None, None, None),
        P("grid", None),
        P(("grid", "rep"), None),
        P(("grid", "rep")),
        P(("grid", "rep"), None, None, None),
        P(("grid", "rep"), None),
    )
    return jax.shard_map(
        shards, mesh=mesh, in_specs=placed, out_specs=P("grid", None, None, None), check_vma=False
    )
```

profile of v0, /device:TPU:1, one launch (start us, length us, event | category | flops | bytes accessed | tf_op | source)
XLA Modules:
  0.0 335.1 jit_solution(412478288045447949)
XLA Ops:
  6.5 2.4 fusion.26
  9.0 4.1 %collective-permute-start.2 = (bf16[6,4,128,128]{3,2,1,0:T(8,128)(2,1)}, bf16[6,4,128,128]{3,2,1,0:T(8,128)(2,1)S(1)}, u32[]{:S(2)}, u32[]{:S(2)}) collective-permute-start(bf16[6,4,128,128]{3,2,1,0:T(8,128)(2,1)} %get-tuple-element.125), channel_id=1, source_target_pairs={{0,2},{2,4},{4,6},{6,8},{8,10},{10,12},{12,14},{14,16},{16,18},{18... | collective-permute-start | bytes 2359304 | tf_op jit(solution)/shard_map/ppermute | solution.py:13
  13.0 1.3 collective-permute-start.3
  14.3 0.8 fusion.27
  15.2 4.0 %collective-permute-start = (s32[6,4]{0,1:T(4,128)S(1)}, s32[6,4]{0,1:T(4,128)S(1)}, u32[]{:S(2)}, u32[]{:S(2)}) collective-permute-start(s32[6,4]{0,1:T(4,128)S(1)} %get-tuple-element.127), channel_id=1, source_target_pairs={{0,2},{2,4},{4,6},{6,8},{8,10},{10,12},{12,14},{14,16},{16,18},{18... | collective-permute-start | bytes 296 | tf_op jit(solution)/shard_map/ppermute | solution.py:13
  19.1 1.3 collective-permute-start.1
  20.4 0.8 copy.20
  21.2 8.3 %collective-permute-done = s32[6,4]{0,1:T(4,128)S(1)} collective-permute-done((s32[6,4]{0,1:T(4,128)S(1)}, s32[6,4]{0,1:T(4,128)S(1)}, u32[]{:S(2)}, u32[]{:S(2)}) %collective-permute-start) | collective-permute-done | bytes 128 | tf_op jit(solution)/shard_map/ppermute | solution.py:13
  29.5 3.6 %collective-permute-done.1 = s32[6,4]{0,1:T(4,128)S(1)} collective-permute-done((s32[6,4]{0,1:T(4,128)S(1)}, s32[6,4]{0,1:T(4,128)S(1)}, u32[]{:S(2)}, u32[]{:S(2)}) %collective-permute-start.1) | collective-permute-done | bytes 128 | tf_op jit(solution)/shard_map/ppermute | solution.py:13
  33.1 0.8 pad_add_fusion
  34.0 5.0 %pad_maximum_fusion = bf16[40,4,128,128]{3,2,1,0:T(8,128)(2,1)} fusion(bf16[6,4,128,128]{3,2,1,0:T(8,128)(2,1)S(1)} %collective-permute-done.3, bf16[28,4,128,128]{3,2,1,0:T(8,128)(2,1)} %param.12, bf16[6,4,128,128]{3,2,1,0:T(8,128)(2,1)S(1)} %collective-permute-done.2), kind=kLoop, calls=%fused_computation.37 | loop fusion | flops 5242880 | bytes 10485760 | tf_op jit(solution)/shard_map/concatenate | solution.py:67
  39.0 5.3 %broadcast_in_dim.2 = f32[40,4,128,128]{3,2,1,0:T(8,128)} broadcast(f32[]{:T(128)} %constant.81.clone.1), dimensions={} | broadcast | bytes 10485764 | tf_op jit(solution)/shard_map/broadcast_in_dim | solution.py:85
  44.3 66.5 %while.12 = (s32[]{:T(128)}, f32[40,4,128,128]{3,2,1,0:T(8,128)}, s32[]{:T(128)}, s32[12,8]{1,0:T(8,128)S(1)}, s32[]{:T(128)}, /*index=5*/s32[40,4]{1,0:T(8,128)...) while((s32[]{:T(128)}, f32[40,4,128,128]{3,2,1,0:T(8,128)}, ...), condition=%wide.region_3.0_spmd, body=%wide.region_0.0_spmd.sunk | while | flops 287574176 | bytes 23076084 | solution.py:86
  45.6 1.0 constant_dynamic-slice_fusion.4
  46.7 3.2 gather_fusion
  51.4 0.7 fusion.50
  52.7 1.8 convolution_bitcast_fusion.5
  54.4 1.9 copy.62
  56.3 4.4 %scatter_fusion = f32[40,4,128,128]{3,2,1,0:T(8,128)} fusion(f32[40,4,128,128]{3,2,1,0:T(8,128)} %get-tuple-element.198, s32[8]{0:T(128)S(1)} %fusion.47, f32[8,4,128,128]{3,2,1,0:T(8,128)S(1)} %copy.62), kind=kCustom, calls=%fused_computation.2.clone.1 | custom fusion | flops 524288 | bytes 6291488 | tf_op jit(solution)/shard_map/while/body/scatter-add | solution.py:83
  62.0 1.0 constant_dynamic-slice_fusion.4
  63.2 3.2 gather_fusion
  67.8 0.7 fusion.50
  69.1 1.8 convolution_bitcast_fusion.5
  70.9 1.9 copy.62
  72.8 4.4 %scatter_fusion = f32[40,4,128,128]{3,2,1,0:T(8,128)} fusion(f32[40,4,128,128]{3,2,1,0:T(8,128)} %get-tuple-element.198, s32[8]{0:T(128)S(1)} %fusion.47, f32[8,4,128,128]{3,2,1,0:T(8,128)S(1)} %copy.62), kind=kCustom, calls=%fused_computation.2.clone.1 | custom fusion | flops 524288 | bytes 6291488 | tf_op jit(solution)/shard_map/while/body/scatter-add | solution.py:83
  78.5 1.0 constant_dynamic-slice_fusion.4
  79.7 3.2 gather_fusion
  84.3 0.7 fusion.50
  85.6 1.8 convolution_bitcast_fusion.5
  87.4 1.9 copy.62
  89.3 4.4 %scatter_fusion = f32[40,4,128,128]{3,2,1,0:T(8,128)} fusion(f32[40,4,128,128]{3,2,1,0:T(8,128)} %get-tuple-element.198, s32[8]{0:T(128)S(1)} %fusion.47, f32[8,4,128,128]{3,2,1,0:T(8,128)S(1)} %copy.62), kind=kCustom, calls=%fused_computation.2.clone.1 | custom fusion | flops 524288 | bytes 6291488 | tf_op jit(solution)/shard_map/while/body/scatter-add | solution.py:83
  94.9 1.0 constant_dynamic-slice_fusion.4
  96.1 3.2 gather_fusion
  100.8 0.7 fusion.50
  102.0 1.8 convolution_bitcast_fusion.5
  103.8 1.9 copy.62
  105.7 4.4 %scatter_fusion = f32[40,4,128,128]{3,2,1,0:T(8,128)} fusion(f32[40,4,128,128]{3,2,1,0:T(8,128)} %get-tuple-element.198, s32[8]{0:T(128)S(1)} %fusion.47, f32[8,4,128,128]{3,2,1,0:T(8,128)S(1)} %copy.62), kind=kCustom, calls=%fused_computation.2.clone.1 | custom fusion | flops 524288 | bytes 6291488 | tf_op jit(solution)/shard_map/while/body/scatter-add | solution.py:83
  110.8 4.8 %copy.23 = f32[2,40,2,128,128]{4,3,2,1,0:T(8,128)S(1)} copy(f32[2,40,2,128,128]{4,3,2,0,1:T(8,128)} %bitcast.73) | data formatting | bytes 20971520 | tf_op jit(solution)/shard_map/transpose | solution.py:18
  115.6 13.3 %all_to_all.5 = f32[2,40,2,128,128]{4,3,2,1,0:T(8,128)} all-to-all(f32[2,40,2,128,128]{4,3,2,1,0:T(8,128)S(1)} %copy.23), channel_id=1, replica_groups=mesh['grid'=128,'rep'=2] {'rep'}, dimensions={0} | all-to-all | bytes 20971520 | tf_op jit(solution)/shard_map/all_to_all | solution.py:23
  128.9 8.0 %reduce_sum.18 = f32[40,2,128,128]{3,2,1,0:T(8,128)} reduce(f32[2,40,2,128,128]{4,3,2,1,0:T(8,128)} %all_to_all.5, f32[]{:T(128)} %constant.81.clone.1), dimensions={0}, to_apply=%region_4.0 | reduce | flops 1310720 | bytes 15728644 | tf_op jit(solution)/shard_map/reduce_sum | solution.py:24
  136.8 1.7 fusion.25
  138.5 3.3 collective-permute-start.4
  141.8 1.6 collective-permute-start.5
  143.4 14.9 %collective-permute-done.4 = f32[6,2,128,128]{3,2,1,0:T(8,128)S(1)} collective-permute-done((f32[6,2,128,128]{3,2,1,0:T(8,128)S(1)}, f32[6,2,128,128]{3,2,1,0:T(8,128)S(1)}, u32[]{:S(2)}, u32[]{:S(2)}) %collective-permute-start.4) | collective-permute-done | bytes 786464 | tf_op jit(solution)/shard_map/ppermute | solution.py:13
  158.3 4.1 %collective-permute-done.5 = f32[6,2,128,128]{3,2,1,0:T(8,128)S(1)} collective-permute-done((f32[6,2,128,128]{3,2,1,0:T(8,128)S(1)}, f32[6,2,128,128]{3,2,1,0:T(8,128)S(1)}, u32[]{:S(2)}, u32[]{:S(2)}) %collective-permute-start.5) | collective-permute-done | bytes 786464 | tf_op jit(solution)/shard_map/ppermute | solution.py:13
  162.6 1.5 convert_element_type.26
  164.2 159.7 %all-gather.2.cloned.1.call-done = bf16[28,4,128,128]{3,2,1,0:T(8,128)(2,1)} async-done(((bf16[28,2,128,128]{3,2,1,0:T(8,128)(2,1)}), bf16[28,4,128,128]{3,2,1,0:T(8,128)(2,1)}) %all-gather.2.cloned.1.call-update) | async-done | bytes 3670032 | tf_op jit(solution)/shard_map/all_gather | solution.py:94
  323.8 4.4 %copy.73 = bf16[28,4,128,128]{3,2,1,0:T(8,128)(2,1)} copy(bf16[28,4,128,128]{3,2,1,0:T(8,128)(2,1)} %all-gather.2.cloned.1.call-done) | data formatting | bytes 7340032
  (47 shorter events, 11.3 us)
Async XLA Ops:
  6.5 317.3 %all-gather.2.cloned.1.call-start = ((), (), s32[]{:S(2)}) async-start(), calls=%async_computation.1 | async-start | bytes 5505024 | tf_op jit(solution)/shard_map/all_gather | solution.py:94
  9.0 25.0 %collective-permute-start.2 = (bf16[6,4,128,128]{3,2,1,0:T(8,128)(2,1)}, bf16[6,4,128,128]{3,2,1,0:T(8,128)(2,1)S(1)}, u32[]{:S(2)}, u32[]{:S(2)}) collective-permute-start(bf16[6,4,128,128]{3,2,1,0:T(8,128)(2,1)} %get-tuple-element.125), channel_id=1, source_target_pairs={{0,2},{2,4},{4,6},{6,8},{8,10},{10,12},{12,14},{14,16},{16,18},{18... | collective-permute-start | bytes 2359304 | tf_op jit(solution)/shard_map/ppermute | solution.py:13
  13.0 20.9 %collective-permute-start.3 = (bf16[6,4,128,128]{3,2,1,0:T(8,128)(2,1)S(1)}, bf16[6,4,128,128]{3,2,1,0:T(8,128)(2,1)S(1)}, u32[]{:S(2)}, u32[]{:S(2)}) collective-permute-start(bf16[6,4,128,128]{3,2,1,0:T(8,128)(2,1)S(1)} %get-tuple-element.126), channel_id=1, source_target_pairs={{2,0},{4,2},{6,4},{8,6},{10,8},{12,10},{14,12},{16,14},{18,16},{20... | collective-permute-start | bytes 2359304 | tf_op jit(solution)/shard_map/ppermute | solution.py:13
  15.2 14.3 %collective-permute-start = (s32[6,4]{0,1:T(4,128)S(1)}, s32[6,4]{0,1:T(4,128)S(1)}, u32[]{:S(2)}, u32[]{:S(2)}) collective-permute-start(s32[6,4]{0,1:T(4,128)S(1)} %get-tuple-element.127), channel_id=1, source_target_pairs={{0,2},{2,4},{4,6},{6,8},{8,10},{10,12},{12,14},{14,16},{16,18},{18... | collective-permute-start | bytes 296 | tf_op jit(solution)/shard_map/ppermute | solution.py:13
  19.1 14.0 %collective-permute-start.1 = (s32[6,4]{0,1:T(4,128)S(1)}, s32[6,4]{0,1:T(4,128)S(1)}, u32[]{:S(2)}, u32[]{:S(2)}) collective-permute-start(s32[6,4]{0,1:T(4,128)S(1)} %get-tuple-element.128), channel_id=1, source_target_pairs={{2,0},{4,2},{6,4},{8,6},{10,8},{12,10},{14,12},{16,14},{18,16},{20... | collective-permute-start | bytes 296 | tf_op jit(solution)/shard_map/ppermute | solution.py:13
  136.8 21.4 %copy-start = (f32[40,2,128,128]{3,2,1,0:T(8,128)S(1)}, f32[40,2,128,128]{3,2,1,0:T(8,128)}, u32[]{:S(2)}) copy-start(f32[40,2,128,128]{3,2,1,0:T(8,128)} %reduce_sum.18) | copy-start | bytes 15728644
  138.5 19.8 %collective-permute-start.4 = (f32[6,2,128,128]{3,2,1,0:T(8,128)S(1)}, f32[6,2,128,128]{3,2,1,0:T(8,128)S(1)}, u32[]{:S(2)}, u32[]{:S(2)}) collective-permute-start(f32[6,2,128,128]{3,2,1,0:T(8,128)S(1)} %get-tuple-element.124), channel_id=1, source_target_pairs={{0,2},{2,4},{4,6},{6,8},{8,10},{10,12},{12,14},{14,16},{16,18},{18... | collective-permute-start | bytes 2359304 | tf_op jit(solution)/shard_map/ppermute | solution.py:13
  141.8 16.5 %slice-start = ((f32[40,2,128,128]{3,2,1,0:T(8,128)}), f32[28,2,128,128]{3,2,1,0:T(8,128)S(1)}, s32[]{:S(2)}) async-start(f32[40,2,128,128]{3,2,1,0:T(8,128)} %reduce_sum.18), calls=%async_computation.2 | async-start | bytes 7340032 | tf_op jit(solution)/shard_map/slice | solution.py:88
  141.8 20.6 %collective-permute-start.5 = (f32[6,2,128,128]{3,2,1,0:T(8,128)S(1)}, f32[6,2,128,128]{3,2,1,0:T(8,128)S(1)}, u32[]{:S(2)}, u32[]{:S(2)}) collective-permute-start(f32[6,2,128,128]{3,2,1,0:T(8,128)S(1)} %get-tuple-element.123), channel_id=1, source_target_pairs={{2,0},{4,2},{6,4},{8,6},{10,8},{12,10},{14,12},{16,14},{18,16},{20... | collective-permute-start | bytes 2359304 | tf_op jit(solution)/shard_map/ppermute | solution.py:13
Sparse Core Ops, SparseCore 0:
  164.3 159.5 all-gather.1
where the time goes:
time: 337 us; the launch traced here: 335 us
  waiting for transfers between devices  191 us (57%)
  local copies, waits for them, and re-layouts  47.8 us (14%)
  other arithmetic  37.7 us (11%)
  starting transfers between devices  15.5 us (5%)
  between operations  13.5 us (4%)
  blocking collectives  13.3 us (4%)
  matrix products  13.2 us (4%)
  loops' own time  3.61 us (1%)
    all_gather x1, waiting for transfers between devices, shards(): lax.all_gather(owned_half.astype(jnp.bfloat16), 'rep', axis=1, tiled=True)  160 us
    ppermute x6, waiting for transfers between devices, shifted(): return lax.ppermute(block, axis, route)  30.8 us
    scatter-add x4, other arithmetic, visit(): return buffer.at[local_rows].add(blocks)  17.6 us
    ppermute x6, starting transfers between devices, shifted(): return lax.ppermute(block, axis, route)  15.5 us
    all_to_all x1, blocking collectives, sum_at_owner(): lax.all_to_all(in_blocks(array, dim, count), axis, 0, 0, tiled=True)  13.3 us
    gather x4, local copies, waits for them, and re-layouts, visit(): window_blocks[local_rows]  12.9 us
    reduce_sum x1, other arithmetic, sum_at_owner(): return jnp.sum(pieces, axis=0)  7.96 us
    transpose x4, local copies, waits for them, and re-layouts, batch_terms(): jnp.einsum('imp,iknp->ikmn', basis_vals, column_scaled, preferred_element...  7.67 us
  transfers between devices with their start and end apart: 7, of which 5 were waited for; matrix products, arithmetic and copies ran while one was open for 1% of the time, Pallas kernels for 0%

commit v1 on v0

--- a/solution.py
+++ b/solution.py
@@ -91,7 +91,12 @@
         gained.append(shifted(halves[low_edge : low_edge + reach], "grid", offset))
     owned_half = owned_half.at[:reach].add(gained[0])
     owned_half = owned_half.at[group_count - reach :].add(gained[1])
-    return lax.all_gather(owned_half.astype(jnp.bfloat16), "rep", axis=1, tiled=True)
+    return jnp.concatenate(
+        lax.all_to_all(
+            jnp.stack([owned_half.astype(jnp.bfloat16)] * lax.axis_size("rep")), "rep", 0, 0
+        ),
+        axis=1,
+    )
 
 
 def solution(mesh):

time: 337 us -> 308 us (0.914)
  the two profiles are of different devices: /device:TPU:1 before, /device:TPU:123 now
where the time goes in v1:
time: 308 us; the launch traced here: 306 us
  blocking collectives  171 us (56%)
  local copies, waits for them, and re-layouts  38.8 us (13%)
  waiting for transfers between devices  31.7 us (10%)
  other arithmetic  31.3 us (10%)
  starting transfers between devices  20.6 us (7%)
  matrix products  9.89 us (3%)
    all_to_all x1, blocking collectives, sum_at_owner(): lax.all_to_all(in_blocks(array, dim, count), axis, 0, 0, tiled=True)  163 us
    ppermute x6, waiting for transfers between devices, shifted(): return lax.ppermute(block, axis, route)  31.7 us
    ppermute x6, starting transfers between devices, shifted(): return lax.ppermute(block, axis, route)  20.6 us
    scatter-add x3, other arithmetic, visit(): return buffer.at[local_rows].add(blocks)  13.2 us
    gather x3, local copies, waits for them, and re-layouts, visit(): window_blocks[local_rows]  9.7 us
    reduce_sum x1, other arithmetic, sum_at_owner(): return jnp.sum(pieces, axis=0)  7.95 us
    all_to_all x1, blocking collectives, shards(): lax.all_to_all(jnp.stack([owned_half.astype(jnp.bfloat16)] * lax.axis_siz...  7.54 us
  transfers between devices with their start and end apart: 6, of which 4 were waited for; matrix products, arithmetic and copies ran while one was open for 1% of the time, Pallas kernels for 0%

profile of v1, /device:TPU:123, one launch (start us, length us, event | category | flops | bytes accessed | tf_op | source)
XLA Modules:
  0.0 305.9 jit_solution(1316232481326029158)
XLA Ops:
  0.0 2.4 fusion.26
  2.4 4.4 %collective-permute-start.2 = (bf16[6,4,128,128]{3,2,1,0:T(8,128)(2,1)}, bf16[6,4,128,128]{3,2,1,0:T(8,128)(2,1)S(1)}, u32[]{:S(2)}, u32[]{:S(2)}) collective-permute-start(bf16[6,4,128,128]{3,2,1,0:T(8,128)(2,1)} %get-tuple-element.125), channel_id=1, source_target_pairs={{0,2},{2,4},{4,6},{6,8},{8,10},{10,12},{12,14},{14,16},{16,18},{18... | collective-permute-start | bytes 2359304 | tf_op jit(solution)/shard_map/ppermute | solution.py:13
  6.8 1.9 collective-permute-start.3
  8.8 0.8 fusion.27
  9.6 6.7 %collective-permute-start = (s32[6,4]{0,1:T(4,128)S(1)}, s32[6,4]{0,1:T(4,128)S(1)}, u32[]{:S(2)}, u32[]{:S(2)}) collective-permute-start(s32[6,4]{0,1:T(4,128)S(1)} %get-tuple-element.127), channel_id=1, source_target_pairs={{0,2},{2,4},{4,6},{6,8},{8,10},{10,12},{12,14},{14,16},{16,18},{18... | collective-permute-start | bytes 296 | tf_op jit(solution)/shard_map/ppermute | solution.py:13
  16.3 1.9 collective-permute-start.1
  18.2 0.8 copy.20
  19.0 4.4 %collective-permute-done = s32[6,4]{0,1:T(4,128)S(1)} collective-permute-done((s32[6,4]{0,1:T(4,128)S(1)}, s32[6,4]{0,1:T(4,128)S(1)}, u32[]{:S(2)}, u32[]{:S(2)}) %collective-permute-start) | collective-permute-done | bytes 128 | tf_op jit(solution)/shard_map/ppermute | solution.py:13
  23.4 6.9 %collective-permute-done.1 = s32[6,4]{0,1:T(4,128)S(1)} collective-permute-done((s32[6,4]{0,1:T(4,128)S(1)}, s32[6,4]{0,1:T(4,128)S(1)}, u32[]{:S(2)}, u32[]{:S(2)}) %collective-permute-start.1) | collective-permute-done | bytes 128 | tf_op jit(solution)/shard_map/ppermute | solution.py:13
  30.2 0.8 pad_add_fusion
  31.1 5.0 %pad_maximum_fusion = bf16[40,4,128,128]{3,2,1,0:T(8,128)(2,1)} fusion(bf16[6,4,128,128]{3,2,1,0:T(8,128)(2,1)S(1)} %collective-permute-done.3, bf16[28,4,128,128]{3,2,1,0:T(8,128)(2,1)} %param.12, bf16[6,4,128,128]{3,2,1,0:T(8,128)(2,1)S(1)} %collective-permute-done.2), kind=kLoop, calls=%fused_computation.37 | loop fusion | flops 5242880 | bytes 10485760 | tf_op jit(solution)/shard_map/concatenate | solution.py:67
  36.1 5.3 %broadcast_in_dim.2 = f32[40,4,128,128]{3,2,1,0:T(8,128)} broadcast(f32[]{:T(128)} %constant.81.clone.1), dimensions={} | broadcast | bytes 10485764 | tf_op jit(solution)/shard_map/broadcast_in_dim | solution.py:85
  41.4 50.0 %while.12 = (s32[]{:T(128)}, f32[40,4,128,128]{3,2,1,0:T(8,128)}, s32[]{:T(128)}, s32[12,8]{1,0:T(8,128)S(1)}, s32[]{:T(128)}, /*index=5*/s32[40,4]{1,0:T(8,128)...) while((s32[]{:T(128)}, f32[40,4,128,128]{3,2,1,0:T(8,128)}, ...), condition=%wide.region_3.0_spmd, body=%wide.region_0.0_spmd.sunk | while | flops 287574176 | bytes 23076084 | solution.py:86
  42.1 0.6 gather_fusion.1
  42.7 1.0 constant_dynamic-slice_fusion.4
  43.9 3.2 %gather_fusion = bf16[8,4,128,128]{3,2,1,0:T(8,128)(2,1)S(1)} fusion(bf16[40,4,128,128]{3,2,1,0:T(8,128)(2,1)} %get-tuple-element.217, s32[1024]{0:T(1024)S(1)} %pad_clamp_fusion.2), kind=kCustom, calls=%fused_computation.1.clone.1 | custom fusion | bytes 2097184 | tf_op jit(solution)/shard_map/while/body/gather | solution.py:77
  47.1 0.6 convolution_convert_fusion.4
  48.5 0.7 fusion.50
  49.2 0.5 convolution_convert_fusion.5
  49.8 1.8 convolution_bitcast_fusion.5
  51.6 1.9 copy.63
  53.5 4.4 %scatter_fusion = f32[40,4,128,128]{3,2,1,0:T(8,128)} fusion(f32[40,4,128,128]{3,2,1,0:T(8,128)} %get-tuple-element.198, s32[8]{0:T(128)S(1)} %fusion.47, f32[8,4,128,128]{3,2,1,0:T(8,128)S(1)} %copy.63), kind=kCustom, calls=%fused_computation.2.clone.1 | custom fusion | flops 524288 | bytes 6291488 | tf_op jit(solution)/shard_map/while/body/scatter-add | solution.py:83
  58.6 0.6 gather_fusion.1
  59.2 1.0 constant_dynamic-slice_fusion.4
  60.3 3.2 %gather_fusion = bf16[8,4,128,128]{3,2,1,0:T(8,128)(2,1)S(1)} fusion(bf16[40,4,128,128]{3,2,1,0:T(8,128)(2,1)} %get-tuple-element.217, s32[1024]{0:T(1024)S(1)} %pad_clamp_fusion.2), kind=kCustom, calls=%fused_computation.1.clone.1 | custom fusion | bytes 2097184 | tf_op jit(solution)/shard_map/while/body/gather | solution.py:77
  63.6 0.6 convolution_convert_fusion.4
  65.0 0.7 fusion.50
  66.3 1.8 convolution_bitcast_fusion.5
  68.0 1.9 copy.63
  69.9 4.4 %scatter_fusion = f32[40,4,128,128]{3,2,1,0:T(8,128)} fusion(f32[40,4,128,128]{3,2,1,0:T(8,128)} %get-tuple-element.198, s32[8]{0:T(128)S(1)} %fusion.47, f32[8,4,128,128]{3,2,1,0:T(8,128)S(1)} %copy.63), kind=kCustom, calls=%fused_computation.2.clone.1 | custom fusion | flops 524288 | bytes 6291488 | tf_op jit(solution)/shard_map/while/body/scatter-add | solution.py:83
  75.1 0.6 gather_fusion.1
  75.6 1.0 constant_dynamic-slice_fusion.4
  76.8 3.2 %gather_fusion = bf16[8,4,128,128]{3,2,1,0:T(8,128)(2,1)S(1)} fusion(bf16[40,4,128,128]{3,2,1,0:T(8,128)(2,1)} %get-tuple-element.217, s32[1024]{0:T(1024)S(1)} %pad_clamp_fusion.2), kind=kCustom, calls=%fused_computation.1.clone.1 | custom fusion | bytes 2097184 | tf_op jit(solution)/shard_map/while/body/gather | solution.py:77
  80.0 0.6 convolution_convert_fusion.4
  81.5 0.7 fusion.50
  82.7 1.8 convolution_bitcast_fusion.5
  84.5 1.9 copy.63
  86.4 4.4 %scatter_fusion = f32[40,4,128,128]{3,2,1,0:T(8,128)} fusion(f32[40,4,128,128]{3,2,1,0:T(8,128)} %get-tuple-element.198, s32[8]{0:T(128)S(1)} %fusion.47, f32[8,4,128,128]{3,2,1,0:T(8,128)S(1)} %copy.63), kind=kCustom, calls=%fused_computation.2.clone.1 | custom fusion | flops 524288 | bytes 6291488 | tf_op jit(solution)/shard_map/while/body/scatter-add | solution.py:83
  91.4 4.8 %copy.23 = f32[2,40,2,128,128]{4,3,2,1,0:T(8,128)S(1)} copy(f32[2,40,2,128,128]{4,3,2,0,1:T(8,128)} %bitcast.78) | data formatting | bytes 20971520 | tf_op jit(solution)/shard_map/transpose | solution.py:18
  96.3 163.1 %all_to_all.10 = f32[2,40,2,128,128]{4,3,2,1,0:T(8,128)} all-to-all(f32[2,40,2,128,128]{4,3,2,1,0:T(8,128)S(1)} %copy.23), channel_id=1, replica_groups=mesh['grid'=128,'rep'=2] {'rep'}, dimensions={0} | all-to-all | bytes 20971520 | tf_op jit(solution)/shard_map/all_to_all | solution.py:23
  259.4 8.0 %reduce_sum.18 = f32[40,2,128,128]{3,2,1,0:T(8,128)} reduce(f32[2,40,2,128,128]{4,3,2,1,0:T(8,128)} %all_to_all.10, f32[]{:T(128)} %constant.81.clone.1), dimensions={0}, to_apply=%region_4.0 | reduce | flops 1310720 | bytes 15728644 | tf_op jit(solution)/shard_map/reduce_sum | solution.py:24
  267.3 1.7 fusion.25
  269.0 2.1 collective-permute-start.4
  271.1 3.6 %collective-permute-start.5 = (f32[6,2,128,128]{3,2,1,0:T(8,128)S(1)}, f32[6,2,128,128]{3,2,1,0:T(8,128)S(1)}, u32[]{:S(2)}, u32[]{:S(2)}) collective-permute-start(f32[6,2,128,128]{3,2,1,0:T(8,128)S(1)} %get-tuple-element.123), channel_id=1, source_target_pairs={{2,0},{4,2},{6,4},{8,6},{10,8},{12,10},{14,12},{16,14},{18,16},{20... | collective-permute-start | bytes 2359304 | tf_op jit(solution)/shard_map/ppermute | solution.py:13
  274.7 15.0 %collective-permute-done.4 = f32[6,2,128,128]{3,2,1,0:T(8,128)S(1)} collective-permute-done((f32[6,2,128,128]{3,2,1,0:T(8,128)S(1)}, f32[6,2,128,128]{3,2,1,0:T(8,128)S(1)}, u32[]{:S(2)}, u32[]{:S(2)}) %collective-permute-start.4) | collective-permute-done | bytes 786464 | tf_op jit(solution)/shard_map/ppermute | solution.py:13
  289.8 5.4 %collective-permute-done.5 = f32[6,2,128,128]{3,2,1,0:T(8,128)S(1)} collective-permute-done((f32[6,2,128,128]{3,2,1,0:T(8,128)S(1)}, f32[6,2,128,128]{3,2,1,0:T(8,128)S(1)}, u32[]{:S(2)}, u32[]{:S(2)}) %collective-permute-start.5) | collective-permute-done | bytes 786464 | tf_op jit(solution)/shard_map/ppermute | solution.py:13
  296.1 7.5 %all_to_all.11 = bf16[2,28,2,128,128]{4,3,2,1,0:T(8,128)(2,1)S(1)} all-to-all(bf16[2,28,2,128,128]{4,3,2,1,0:T(8,128)(2,1)S(1)} %pad_maximum_fusion.1), channel_id=1, replica_groups=mesh['grid'=128,'rep'=2] {'rep'}, dimensions={0} | all-to-all | bytes 7340032 | tf_op jit(solution)/shard_map/all_to_all | solution.py:95
  303.6 2.3 copy.24
  (31 shorter events, 5.3 us)
Async XLA Ops:
  2.4 28.7 %collective-permute-start.2 = (bf16[6,4,128,128]{3,2,1,0:T(8,128)(2,1)}, bf16[6,4,128,128]{3,2,1,0:T(8,128)(2,1)S(1)}, u32[]{:S(2)}, u32[]{:S(2)}) collective-permute-start(bf16[6,4,128,128]{3,2,1,0:T(8,128)(2,1)} %get-tuple-element.125), channel_id=1, source_target_pairs={{0,2},{2,4},{4,6},{6,8},{8,10},{10,12},{12,14},{14,16},{16,18},{18... | collective-permute-start | bytes 2359304 | tf_op jit(solution)/shard_map/ppermute | solution.py:13
  6.8 24.3 %collective-permute-start.3 = (bf16[6,4,128,128]{3,2,1,0:T(8,128)(2,1)S(1)}, bf16[6,4,128,128]{3,2,1,0:T(8,128)(2,1)S(1)}, u32[]{:S(2)}, u32[]{:S(2)}) collective-permute-start(bf16[6,4,128,128]{3,2,1,0:T(8,128)(2,1)S(1)} %get-tuple-element.126), channel_id=1, source_target_pairs={{2,0},{4,2},{6,4},{8,6},{10,8},{12,10},{14,12},{16,14},{18,16},{20... | collective-permute-start | bytes 2359304 | tf_op jit(solution)/shard_map/ppermute | solution.py:13
  9.6 13.8 %collective-permute-start = (s32[6,4]{0,1:T(4,128)S(1)}, s32[6,4]{0,1:T(4,128)S(1)}, u32[]{:S(2)}, u32[]{:S(2)}) collective-permute-start(s32[6,4]{0,1:T(4,128)S(1)} %get-tuple-element.127), channel_id=1, source_target_pairs={{0,2},{2,4},{4,6},{6,8},{8,10},{10,12},{12,14},{14,16},{16,18},{18... | collective-permute-start | bytes 296 | tf_op jit(solution)/shard_map/ppermute | solution.py:13
  16.3 14.0 %collective-permute-start.1 = (s32[6,4]{0,1:T(4,128)S(1)}, s32[6,4]{0,1:T(4,128)S(1)}, u32[]{:S(2)}, u32[]{:S(2)}) collective-permute-start(s32[6,4]{0,1:T(4,128)S(1)} %get-tuple-element.128), channel_id=1, source_target_pairs={{2,0},{4,2},{6,4},{8,6},{10,8},{12,10},{14,12},{16,14},{18,16},{20... | collective-permute-start | bytes 296 | tf_op jit(solution)/shard_map/ppermute | solution.py:13
  267.3 22.4 %copy-start = (f32[40,2,128,128]{3,2,1,0:T(8,128)S(1)}, f32[40,2,128,128]{3,2,1,0:T(8,128)}, u32[]{:S(2)}) copy-start(f32[40,2,128,128]{3,2,1,0:T(8,128)} %reduce_sum.18) | copy-start | bytes 15728644
  269.0 20.8 %collective-permute-start.4 = (f32[6,2,128,128]{3,2,1,0:T(8,128)S(1)}, f32[6,2,128,128]{3,2,1,0:T(8,128)S(1)}, u32[]{:S(2)}, u32[]{:S(2)}) collective-permute-start(f32[6,2,128,128]{3,2,1,0:T(8,128)S(1)} %get-tuple-element.124), channel_id=1, source_target_pairs={{0,2},{2,4},{4,6},{6,8},{8,10},{10,12},{12,14},{14,16},{16,18},{18... | collective-permute-start | bytes 2359304 | tf_op jit(solution)/shard_map/ppermute | solution.py:13
  271.0 18.7 %slice-start = ((f32[40,2,128,128]{3,2,1,0:T(8,128)}), f32[28,2,128,128]{3,2,1,0:T(8,128)S(1)}, s32[]{:S(2)}) async-start(f32[40,2,128,128]{3,2,1,0:T(8,128)} %reduce_sum.18), calls=%async_computation.2 | async-start | bytes 7340032 | tf_op jit(solution)/shard_map/slice | solution.py:88
  271.1 24.2 %collective-permute-start.5 = (f32[6,2,128,128]{3,2,1,0:T(8,128)S(1)}, f32[6,2,128,128]{3,2,1,0:T(8,128)S(1)}, u32[]{:S(2)}, u32[]{:S(2)}) collective-permute-start(f32[6,2,128,128]{3,2,1,0:T(8,128)S(1)} %get-tuple-element.123), channel_id=1, source_target_pairs={{2,0},{4,2},{6,4},{8,6},{10,8},{12,10},{14,12},{16,14},{18,16},{20... | collective-permute-start | bytes 2359304 | tf_op jit(solution)/shard_map/ppermute | solution.py:13
